TPU v7x, 32 devices: a whole 2x2x4 slice. The times are simulated.
32 devices in a mesh: depth: 8 (over y, x, core), dp: 4 (over z).
Axes of the slice: x: 2, y: 2, z: 4, core: 2. Of those that a mesh axis runs over, the one named last changes fastest.
Arguments:
- token_ids: int32 [512], P('dp'), may hold values from 0 to 10239
- embedding: bfloat16 [10240, 512], P('depth'), may hold values from -6 to 6
- w_up: bfloat16 [16, 512, 2048], P('depth'), may hold values from -0.25 to 0.25
- w_down: bfloat16 [16, 2048, 512], P('depth'), may hold values from -0.125 to 0.125
- cotangent: bfloat16 [512, 512], P('dp'), may hold values from -0.119628906 to 0.119628906
Outputs:
- grad_up: float32 [16, 512, 2048], P('depth', 'dp')
- grad_down: float32 [16, 2048, 512], P('depth', 'dp')
All inputs are finite; a program needn't handle non-finite values.
Results may differ from a plain program's by a relative error of at most 0.03.
Values may be sent and summed in bfloat16 or wider, within the bound.
No kernel may reach another device: no remote copies, remote signals or barrier semaphores. Data moves between devices by JAX's collectives and lax.ppermute only.
A program may use at most 64 MiB of HBM per device.

v0:
```python
import jax
import jax.numpy as jnp
from jax import lax
from jax.sharding import PartitionSpec as P

RELAX = 3
EPSILON = 1e-06
GAMMA = 0.05


def shifted(block, axis, distance):
    devices = range(lax.axis_size(axis))
    route = [(i - distance, i) for i in devices if i - distance in devices]
    return lax.ppermute(block, axis, route)


def layer_forward(state, weight_up, weight_down):
    scale = lax.rsqrt(jnp.mean(state * state, axis=-1, keepdims=True) + EPSILON)
    normed = (state * scale).astype(jnp.bfloat16)
    before = jnp.dot(normed, weight_up, preferred_element_type=jnp.float32)
    hidden = jax.nn.silu(before).astype(jnp.bfloat16)
    output = state + jnp.dot(hidden, weight_down, preferred_element_type=jnp.float32)
    return (output, (scale, normed, before, hidden))


def layer_adjoint(state, saved, adjoint, weight_up, weight_down):
    scale, normed, before, hidden = saved
    adjoint_low = adjoint.astype(jnp.bfloat16)
    toward_hidden = lax.dot_general(
        adjoint_low, weight_down, (((1,), (1,)), ((), ())), preferred_element_type=jnp.float32
    )
    sigma = jax.nn.sigmoid(before)
    delta = (toward_hidden * sigma * (1.0 + before * (1.0 - sigma))).astype(jnp.bfloat16)
    toward_normed = lax.dot_general(
        delta, weight_up, (((1,), (1,)), ((), ())), preferred_element_type=jnp.float32
    )
    unit = state * scale
    inner = jnp.mean(toward_normed * unit, axis=-1, keepdims=True)
    return (adjoint + scale * (toward_normed - unit * inner), adjoint_low, delta)


def coarse_matrix(weight_up, weight_down):
    total = jnp.dot(weight_up[0], weight_down[0], preferred_element_type=jnp.float32)
    total = total + jnp.dot(weight_up[1], weight_down[1], preferred_element_type=jnp.float32)
    return jnp.eye(weight_up.shape[1], dtype=jnp.float32) + GAMMA * total


def shards(token_ids, embedding, w_up, w_down, cotangent):
    depth = lax.axis_size("depth")
    position = lax.axis_index("depth")
    first = position == 0
    final_block = position == depth - 1
    layers = w_up.shape[0]
    vocab_rows = embedding.shape[0]
    local_ids = token_ids - position * vocab_rows
    inside = (local_ids >= 0) & (local_ids < vocab_rows)
    picked = jnp.take(embedding, jnp.clip(local_ids, 0, vocab_rows - 1), axis=0)
    picked = jnp.where(inside[:, None], picked, jnp.zeros_like(picked)).astype(jnp.float32)
    start = lax.psum(picked.astype(jnp.bfloat16), "depth").astype(jnp.float32)
    matrix = coarse_matrix(w_up, w_down)
    transposed = matrix.T
    zeros = jnp.zeros_like(start)
    coarse = start
    arrived_projection = zeros
    for sweep in range(RELAX):
        run_state = coarse
        for run_layer in range(layers):
            run_state, unused = layer_forward(run_state, w_up[run_layer], w_down[run_layer])
        projection = jnp.dot(coarse, matrix, precision=lax.Precision.HIGHEST)
        arrived, arrived_projection = shifted((run_state, projection), "depth", 1)
        coarse = jnp.where(first, start, arrived)
    tau = coarse - arrived_projection

    def forward_turn(turn, incoming):
        carried = jnp.dot(incoming + tau, matrix, precision=lax.Precision.HIGHEST)
        return shifted(carried.astype(jnp.bfloat16), "depth", 1).astype(carried.dtype)

    incoming = lax.fori_loop(0, depth - 1, forward_turn, zeros)
    corrected = incoming + tau
    states = []
    saves = []
    state = corrected
    for layer in range(layers):
        states.append(state)
        state, saved = layer_forward(state, w_up[layer], w_down[layer])
        saves.append(saved)

    def run_adjoint(adjoint):
        for layer in reversed(range(layers)):
            adjoint, low, delta = layer_adjoint(
                states[layer], saves[layer], adjoint, w_up[layer], w_down[layer]
            )
        return adjoint

    final = cotangent.astype(jnp.float32)
    adjoint_state = final
    back_projection = zeros
    for sweep in range(RELAX):
        begun = run_adjoint(adjoint_state)
        projection = jnp.dot(adjoint_state, transposed, precision=lax.Precision.HIGHEST)
        arrived, back_projection = (
            shifted(begun.astype(jnp.bfloat16), "depth", -1).astype(begun.dtype),
            shifted(projection.astype(jnp.bfloat16), "depth", -1).astype(projection.dtype),
        )
        adjoint_state = jnp.where(final_block, final, arrived)
    back_tau = adjoint_state - back_projection

    def backward_turn(turn, incoming):
        carried = jnp.dot(incoming + back_tau, transposed, precision=lax.Precision.HIGHEST)
        return shifted(carried.astype(jnp.bfloat16), "depth", -1).astype(carried.dtype)

    back_incoming = lax.fori_loop(0, depth - 1, backward_turn, zeros)
    adjoint = back_incoming + back_tau
    lows = [None] * layers
    deltas = [None] * layers
    for layer in reversed(range(layers)):
        adjoint, low, delta = layer_adjoint(
            states[layer], saves[layer], adjoint, w_up[layer], w_down[layer]
        )
        lows[layer] = low
        deltas[layer] = delta
    normed_all = jnp.stack([saves[layer][1] for layer in range(layers)], 0)
    hidden_all = jnp.stack([saves[layer][3] for layer in range(layers)], 0)
    delta_all = jnp.stack(deltas, 0)
    low_all = jnp.stack(lows, 0)
    normed_part, hidden_part = (
        lax.all_to_all(normed_all, "dp", split_axis=2, concat_axis=1, tiled=True),
        lax.all_to_all(hidden_all, "dp", split_axis=2, concat_axis=1, tiled=True),
    )
    delta_whole, low_whole = (
        lax.all_gather(delta_all, "dp", axis=1, tiled=True),
        lax.all_gather(low_all, "dp", axis=1, tiled=True),
    )
    grad_up = jnp.einsum(
        "ltd,ltf->ldf", normed_part, delta_whole, preferred_element_type=jnp.float32
    )
    grad_down = jnp.einsum(
        "ltf,ltd->lfd", hidden_part, low_whole, preferred_element_type=jnp.float32
    )
    return (grad_up, grad_down)


def solution(mesh):
    in_specs = (
        P("dp"),
        P("depth", None),
        P("depth", None, None),
        P("depth", None, None),
        P("dp", None),
    )
    out_specs = (P("depth", "dp", None), P("depth", "dp", None))
    return jax.shard_map(shards, mesh=mesh, in_specs=in_specs, out_specs=out_specs, check_vma=False)
```

profile of v0, /device:TPU:0, one launch (start us, length us, event | category | flops | bytes accessed | tf_op | source)
XLA Modules:
  0.0 437.5 jit_solution(14068713169038172877)
XLA Ops:
  10.2 57.6 %all-reduce.2.cloned.1.call-done = bf16[128,512]{1,0:T(8,128)(2,1)} async-done(((bf16[128,512]{1,0:T(8,128)(2,1)}), bf16[128,512]{1,0:T(8,128)(2,1)}) %all-reduce.2.cloned.1.call-update) | async-done | bytes 131088 | tf_op jit(solution)/shard_map/psum | solution.py:59
  76.4 4.4 %fusion.27 = f32[512,512]{1,0:T(8,128)} fusion(bf16[2,2048,512]{2,1,0:T(8,128)(2,1)} %param.12, bf16[2,512,2048]{2,1,0:T(8,128)(2,1)} %param.11), kind=kOutput, calls=%fused_computation.40 | convolution fusion | flops 1073741824 | bytes 5242880 | tf_op jit(solution)/shard_map/dot_general | solution.py:44
  103.6 4.0 collective-permute-start.4
  109.1 4.5 %collective-permute-start.5 = (f32[128,512]{1,0:T(8,128)}, f32[128,512]{1,0:T(8,128)S(1)}, u32[]{:S(2)}, u32[]{:S(2)}) collective-permute-start(f32[128,512]{1,0:T(8,128)} %fusion.244), channel_id=1, source_target_pairs={{0,4},{4,8},{8,12},{12,16},{16,20},{20,24},{24,28},{1,5},{5,9},{9,... | collective-permute-start | bytes 786440 | tf_op jit(solution)/shard_map/ppermute | solution.py:14
  114.8 50.3 %while.22 = (s32[]{:T(128)}, f32[128,512]{1,0:T(8,128)S(1)}, f32[128,512]{1,0:T(8,128)S(1)}, f32[512,512]{1,0:T(8,128)S(1)}, s32[]{:T(128)}, /*index=5*/s32[]{:T(128)}) while((s32[]{:T(128)}, f32[128,512]{1,0:T(8,128)S(1)}, f32[128,512]{1,0:T(8,128)S(1)}, f32[512,512]{1,0:T(8,128)S(1)}, s32[]{:T(128)}, /*index=5*/s32[]{:T(128)}) %tuple.64), condition=%wide.region_8.9_spmd.clone, body=%wide.region_7.8_spmd.clone.sunk | while | flops 402915328 | bytes 2621559 | solution.py:78
  115.6 5.4 %collective-permute-start = (bf16[128,512]{1,0:T(8,128)(2,1)S(1)}, bf16[128,512]{1,0:T(8,128)(2,1)S(1)}, u32[]{:S(2)}, u32[]{:S(2)}) collective-permute-start(bf16[128,512]{1,0:T(8,128)(2,1)S(1)} %convolution_convert_fusion.5), channel_id=1, source_target_pairs={{0,4},{4,8},{8,12},{12,16},{16,20},{20,24},{24,28},{1,5},{5,9},{9,... | collective-permute-start | bytes 393224 | tf_op jit(solution)/shard_map/while/body/eval_jaxpr/ppermute | solution.py:14
  122.8 5.2 %collective-permute-start = (bf16[128,512]{1,0:T(8,128)(2,1)S(1)}, bf16[128,512]{1,0:T(8,128)(2,1)S(1)}, u32[]{:S(2)}, u32[]{:S(2)}) collective-permute-start(bf16[128,512]{1,0:T(8,128)(2,1)S(1)} %convolution_convert_fusion.5), channel_id=1, source_target_pairs={{0,4},{4,8},{8,12},{12,16},{16,20},{20,24},{24,28},{1,5},{5,9},{9,... | collective-permute-start | bytes 393224 | tf_op jit(solution)/shard_map/while/body/eval_jaxpr/ppermute | solution.py:14
  129.8 5.3 %collective-permute-start = (bf16[128,512]{1,0:T(8,128)(2,1)S(1)}, bf16[128,512]{1,0:T(8,128)(2,1)S(1)}, u32[]{:S(2)}, u32[]{:S(2)}) collective-permute-start(bf16[128,512]{1,0:T(8,128)(2,1)S(1)} %convolution_convert_fusion.5), channel_id=1, source_target_pairs={{0,4},{4,8},{8,12},{12,16},{16,20},{20,24},{24,28},{1,5},{5,9},{9,... | collective-permute-start | bytes 393224 | tf_op jit(solution)/shard_map/while/body/eval_jaxpr/ppermute | solution.py:14
  136.8 5.3 %collective-permute-start = (bf16[128,512]{1,0:T(8,128)(2,1)S(1)}, bf16[128,512]{1,0:T(8,128)(2,1)S(1)}, u32[]{:S(2)}, u32[]{:S(2)}) collective-permute-start(bf16[128,512]{1,0:T(8,128)(2,1)S(1)} %convolution_convert_fusion.5), channel_id=1, source_target_pairs={{0,4},{4,8},{8,12},{12,16},{16,20},{20,24},{24,28},{1,5},{5,9},{9,... | collective-permute-start | bytes 393224 | tf_op jit(solution)/shard_map/while/body/eval_jaxpr/ppermute | solution.py:14
  143.9 5.3 %collective-permute-start = (bf16[128,512]{1,0:T(8,128)(2,1)S(1)}, bf16[128,512]{1,0:T(8,128)(2,1)S(1)}, u32[]{:S(2)}, u32[]{:S(2)}) collective-permute-start(bf16[128,512]{1,0:T(8,128)(2,1)S(1)} %convolution_convert_fusion.5), channel_id=1, source_target_pairs={{0,4},{4,8},{8,12},{12,16},{16,20},{20,24},{24,28},{1,5},{5,9},{9,... | collective-permute-start | bytes 393224 | tf_op jit(solution)/shard_map/while/body/eval_jaxpr/ppermute | solution.py:14
  151.0 5.3 %collective-permute-start = (bf16[128,512]{1,0:T(8,128)(2,1)S(1)}, bf16[128,512]{1,0:T(8,128)(2,1)S(1)}, u32[]{:S(2)}, u32[]{:S(2)}) collective-permute-start(bf16[128,512]{1,0:T(8,128)(2,1)S(1)} %convolution_convert_fusion.5), channel_id=1, source_target_pairs={{0,4},{4,8},{8,12},{12,16},{16,20},{20,24},{24,28},{1,5},{5,9},{9,... | collective-permute-start | bytes 393224 | tf_op jit(solution)/shard_map/while/body/eval_jaxpr/ppermute | solution.py:14
  158.1 6.1 %collective-permute-start = (bf16[128,512]{1,0:T(8,128)(2,1)S(1)}, bf16[128,512]{1,0:T(8,128)(2,1)S(1)}, u32[]{:S(2)}, u32[]{:S(2)}) collective-permute-start(bf16[128,512]{1,0:T(8,128)(2,1)S(1)} %convolution_convert_fusion.5), channel_id=1, source_target_pairs={{0,4},{4,8},{8,12},{12,16},{16,20},{20,24},{24,28},{1,5},{5,9},{9,... | collective-permute-start | bytes 393224 | tf_op jit(solution)/shard_map/while/body/eval_jaxpr/ppermute | solution.py:14
  172.0 4.2 multiply_reduce_fusion.6
  181.6 5.7 %collective-permute-done.6 = bf16[128,512]{1,0:T(8,128)(2,1)S(1)} collective-permute-done((bf16[128,512]{1,0:T(8,128)(2,1)S(1)}, bf16[128,512]{1,0:T(8,128)(2,1)S(1)}, u32[]{:S(2)}, u32[]{:S(2)}) %collective-permute-start.6) | collective-permute-done | bytes 131104 | tf_op jit(solution)/shard_map/ppermute | solution.py:14
  187.4 4.2 multiply_reduce_fusion.4
  191.7 4.3 multiply_reduce_fusion.3
  197.4 6.6 %collective-permute-done.7 = bf16[128,512]{1,0:T(8,128)(2,1)S(1)} collective-permute-done((bf16[128,512]{1,0:T(8,128)(2,1)S(1)}, bf16[128,512]{1,0:T(8,128)(2,1)S(1)}, u32[]{:S(2)}, u32[]{:S(2)}) %collective-permute-start.7) | collective-permute-done | bytes 131104 | tf_op jit(solution)/shard_map/ppermute | solution.py:14
  207.1 4.8 %multiply_reduce_fusion.2 = (f32[128]{0:T(128)S(1)}, f32[128,512]{1,0:T(8,128)}) fusion(f32[128,512]{1,0:T(8,128)S(1)} %get-tuple-element.122, f32[128]{0:T(128)S(1)} %add_rsqrt_fusion, bf16[2,512,2048]{2,1,0:T(8,128)(2,1)} %param.11, f32[128,2048]{1,0:T(8,128)} %fusion.43, bf16[2,2048,512]{2,1,0:T(8,128)(2,1)} %param.12, ...), kind=kOutput, calls=%fused_computation.173 | convolution fusion | flops 539688832 | bytes 6030337 | tf_op jit(solution)/shard_map/dot_general | solution.py:34
  213.0 4.2 multiply_reduce_fusion.1
  226.9 56.5 %while.23 = (s32[]{:T(128)}, f32[128,512]{1,0:T(8,128)S(1)}, f32[128,512]{1,0:T(8,128)S(1)}, f32[512,512]{1,0:T(8,128)S(1)}, s32[]{:T(128)}, /*index=5*/s32[]{:T(128)}) while((s32[]{:T(128)}, f32[128,512]{1,0:T(8,128)S(1)}, f32[128,512]{1,0:T(8,128)S(1)}, f32[512,512]{1,0:T(8,128)S(1)}, s32[]{:T(128)}, ...), condition=%wide.region_18.19_spmd.clone, body=%wide.region_17.18_spmd.clone.sunk | while | flops 402915328 | bytes 2621559 | solution.py:112
  228.9 6.6 %collective-permute-done.1 = bf16[128,512]{1,0:T(8,128)(2,1)S(1)} collective-permute-done((bf16[128,512]{1,0:T(8,128)(2,1)S(1)}, bf16[128,512]{1,0:T(8,128)(2,1)S(1)}, u32[]{:S(2)}, u32[]{:S(2)}) %collective-permute-start.1) | collective-permute-done | bytes 131104 | tf_op jit(solution)/shard_map/while/body/eval_jaxpr/ppermute | solution.py:14
  237.6 5.9 %collective-permute-done.1 = bf16[128,512]{1,0:T(8,128)(2,1)S(1)} collective-permute-done((bf16[128,512]{1,0:T(8,128)(2,1)S(1)}, bf16[128,512]{1,0:T(8,128)(2,1)S(1)}, u32[]{:S(2)}, u32[]{:S(2)}) %collective-permute-start.1) | collective-permute-done | bytes 131104 | tf_op jit(solution)/shard_map/while/body/eval_jaxpr/ppermute | solution.py:14
  245.6 5.9 %collective-permute-done.1 = bf16[128,512]{1,0:T(8,128)(2,1)S(1)} collective-permute-done((bf16[128,512]{1,0:T(8,128)(2,1)S(1)}, bf16[128,512]{1,0:T(8,128)(2,1)S(1)}, u32[]{:S(2)}, u32[]{:S(2)}) %collective-permute-start.1) | collective-permute-done | bytes 131104 | tf_op jit(solution)/shard_map/while/body/eval_jaxpr/ppermute | solution.py:14
  253.5 5.9 %collective-permute-done.1 = bf16[128,512]{1,0:T(8,128)(2,1)S(1)} collective-permute-done((bf16[128,512]{1,0:T(8,128)(2,1)S(1)}, bf16[128,512]{1,0:T(8,128)(2,1)S(1)}, u32[]{:S(2)}, u32[]{:S(2)}) %collective-permute-start.1) | collective-permute-done | bytes 131104 | tf_op jit(solution)/shard_map/while/body/eval_jaxpr/ppermute | solution.py:14
  261.5 5.9 %collective-permute-done.1 = bf16[128,512]{1,0:T(8,128)(2,1)S(1)} collective-permute-done((bf16[128,512]{1,0:T(8,128)(2,1)S(1)}, bf16[128,512]{1,0:T(8,128)(2,1)S(1)}, u32[]{:S(2)}, u32[]{:S(2)}) %collective-permute-start.1) | collective-permute-done | bytes 131104 | tf_op jit(solution)/shard_map/while/body/eval_jaxpr/ppermute | solution.py:14
  269.5 5.9 %collective-permute-done.1 = bf16[128,512]{1,0:T(8,128)(2,1)S(1)} collective-permute-done((bf16[128,512]{1,0:T(8,128)(2,1)S(1)}, bf16[128,512]{1,0:T(8,128)(2,1)S(1)}, u32[]{:S(2)}, u32[]{:S(2)}) %collective-permute-start.1) | collective-permute-done | bytes 131104 | tf_op jit(solution)/shard_map/while/body/eval_jaxpr/ppermute | solution.py:14
  277.4 5.9 %collective-permute-done.1 = bf16[128,512]{1,0:T(8,128)(2,1)S(1)} collective-permute-done((bf16[128,512]{1,0:T(8,128)(2,1)S(1)}, bf16[128,512]{1,0:T(8,128)(2,1)S(1)}, u32[]{:S(2)}, u32[]{:S(2)}) %collective-permute-start.1) | collective-permute-done | bytes 131104 | tf_op jit(solution)/shard_map/while/body/eval_jaxpr/ppermute | solution.py:14
  296.1 4.6 %all-to-all-start = ((bf16[2,128,512]{1,0,2:T(2,128)(2,1)}), bf16[2,128,512]{1,0,2:T(2,128)(2,1)}, u32[]{:S(2)}, u32[]{:S(2)}) async-start(bf16[2,128,512]{1,0,2:T(2,128)(2,1)} %copy.10), calls=%async_computation | async-start | bytes 524288 | tf_op jit(solution)/shard_map/all_to_all | solution.py:127
  303.4 4.2 all-to-all-done
  313.1 37.0 %all-to-all-done.1 = bf16[2,128,2048]{1,0,2:T(2,128)(2,1)S(1)} async-done(((bf16[2,128,2048]{1,0,2:T(2,128)(2,1)}), bf16[2,128,2048]{1,0,2:T(2,128)(2,1)S(1)}, u32[]{:S(2)}, u32[]{:S(2)}) %all-to-all-start.1) | async-done | bytes 1048608 | tf_op jit(solution)/shard_map/all_to_all | solution.py:128
  354.8 72.0 %all-gather.3.cloned.1.call-done = bf16[2,512,2048]{2,1,0:T(8,128)(2,1)} async-done(((bf16[2,128,2048]{2,1,0:T(8,128)(2,1)}), bf16[2,512,2048]{2,1,0:T(8,128)(2,1)}) %all-gather.3.cloned.1.call-update) | async-done | bytes 4194320 | tf_op jit(solution)/shard_map/all_gather | solution.py:131
  426.8 4.2 fusion.291
  (158 shorter events, 116.3 us)
Async XLA Ops:
  7.2 60.6 %all-reduce.2.cloned.1.call-start = ((), (), s32[]{:S(2)}) async-start(), calls=%async_computation.2 | async-start | bytes 262144 | tf_op jit(solution)/shard_map/psum | solution.py:59
  10.1 341.2 %all-gather.5.cloned.1.call-start = ((), (), s32[]{:S(2)}) async-start(), calls=%async_computation.4 | async-start | bytes 1310720 | tf_op jit(solution)/shard_map/all_gather | solution.py:132
  75.0 5.9 %collective-permute-start.2 = (f32[128,512]{1,0:T(8,128)S(1)}, f32[128,512]{1,0:T(8,128)S(1)}, u32[]{:S(2)}, u32[]{:S(2)}) collective-permute-start(f32[128,512]{1,0:T(8,128)S(1)} %fusion.115), channel_id=1, source_target_pairs={{0,4},{4,8},{8,12},{12,16},{16,20},{20,24},{24,28},{1,5},{5,9},{9,... | collective-permute-start | bytes 786440 | tf_op jit(solution)/shard_map/ppermute | solution.py:14
  87.8 7.2 %collective-permute-start.3 = (f32[128,512]{1,0:T(8,128)}, f32[128,512]{1,0:T(8,128)S(1)}, u32[]{:S(2)}, u32[]{:S(2)}) collective-permute-start(f32[128,512]{1,0:T(8,128)} %fusion.118), channel_id=1, source_target_pairs={{0,4},{4,8},{8,12},{12,16},{16,20},{20,24},{24,28},{1,5},{5,9},{9,... | collective-permute-start | bytes 786440 | tf_op jit(solution)/shard_map/ppermute | solution.py:14
  95.0 12.6 %copy-start.1 = (f32[512,512]{1,0:T(8,128)}, f32[512,512]{1,0:T(8,128)S(1)}, u32[]{:S(2)}) copy-start(f32[512,512]{1,0:T(8,128)S(1)} %get-tuple-element.120) | copy-start | bytes 3145732
  103.6 10.0 %collective-permute-start.4 = (f32[128,512]{1,0:T(8,128)}, f32[128,512]{1,0:T(8,128)}, u32[]{:S(2)}, u32[]{:S(2)}) collective-permute-start(f32[128,512]{1,0:T(8,128)} %fusion.121), channel_id=1, source_target_pairs={{0,4},{4,8},{8,12},{12,16},{16,20},{20,24},{24,28},{1,5},{5,9},{9,... | collective-permute-start | bytes 786440 | tf_op jit(solution)/shard_map/ppermute | solution.py:14
  109.1 5.7 %collective-permute-start.5 = (f32[128,512]{1,0:T(8,128)}, f32[128,512]{1,0:T(8,128)S(1)}, u32[]{:S(2)}, u32[]{:S(2)}) collective-permute-start(f32[128,512]{1,0:T(8,128)} %fusion.244), channel_id=1, source_target_pairs={{0,4},{4,8},{8,12},{12,16},{16,20},{20,24},{24,28},{1,5},{5,9},{9,... | collective-permute-start | bytes 786440 | tf_op jit(solution)/shard_map/ppermute | solution.py:14
  115.6 6.4 %collective-permute-start = (bf16[128,512]{1,0:T(8,128)(2,1)S(1)}, bf16[128,512]{1,0:T(8,128)(2,1)S(1)}, u32[]{:S(2)}, u32[]{:S(2)}) collective-permute-start(bf16[128,512]{1,0:T(8,128)(2,1)S(1)} %convolution_convert_fusion.5), channel_id=1, source_target_pairs={{0,4},{4,8},{8,12},{12,16},{16,20},{20,24},{24,28},{1,5},{5,9},{9,... | collective-permute-start | bytes 393224 | tf_op jit(solution)/shard_map/while/body/eval_jaxpr/ppermute | solution.py:14
  122.8 6.2 %collective-permute-start = (bf16[128,512]{1,0:T(8,128)(2,1)S(1)}, bf16[128,512]{1,0:T(8,128)(2,1)S(1)}, u32[]{:S(2)}, u32[]{:S(2)}) collective-permute-start(bf16[128,512]{1,0:T(8,128)(2,1)S(1)} %convolution_convert_fusion.5), channel_id=1, source_target_pairs={{0,4},{4,8},{8,12},{12,16},{16,20},{20,24},{24,28},{1,5},{5,9},{9,... | collective-permute-start | bytes 393224 | tf_op jit(solution)/shard_map/while/body/eval_jaxpr/ppermute | solution.py:14
  129.8 6.3 %collective-permute-start = (bf16[128,512]{1,0:T(8,128)(2,1)S(1)}, bf16[128,512]{1,0:T(8,128)(2,1)S(1)}, u32[]{:S(2)}, u32[]{:S(2)}) collective-permute-start(bf16[128,512]{1,0:T(8,128)(2,1)S(1)} %convolution_convert_fusion.5), channel_id=1, source_target_pairs={{0,4},{4,8},{8,12},{12,16},{16,20},{20,24},{24,28},{1,5},{5,9},{9,... | collective-permute-start | bytes 393224 | tf_op jit(solution)/shard_map/while/body/eval_jaxpr/ppermute | solution.py:14
  136.8 6.3 %collective-permute-start = (bf16[128,512]{1,0:T(8,128)(2,1)S(1)}, bf16[128,512]{1,0:T(8,128)(2,1)S(1)}, u32[]{:S(2)}, u32[]{:S(2)}) collective-permute-start(bf16[128,512]{1,0:T(8,128)(2,1)S(1)} %convolution_convert_fusion.5), channel_id=1, source_target_pairs={{0,4},{4,8},{8,12},{12,16},{16,20},{20,24},{24,28},{1,5},{5,9},{9,... | collective-permute-start | bytes 393224 | tf_op jit(solution)/shard_map/while/body/eval_jaxpr/ppermute | solution.py:14
  143.9 6.3 %collective-permute-start = (bf16[128,512]{1,0:T(8,128)(2,1)S(1)}, bf16[128,512]{1,0:T(8,128)(2,1)S(1)}, u32[]{:S(2)}, u32[]{:S(2)}) collective-permute-start(bf16[128,512]{1,0:T(8,128)(2,1)S(1)} %convolution_convert_fusion.5), channel_id=1, source_target_pairs={{0,4},{4,8},{8,12},{12,16},{16,20},{20,24},{24,28},{1,5},{5,9},{9,... | collective-permute-start | bytes 393224 | tf_op jit(solution)/shard_map/while/body/eval_jaxpr/ppermute | solution.py:14
  151.0 6.3 %collective-permute-start = (bf16[128,512]{1,0:T(8,128)(2,1)S(1)}, bf16[128,512]{1,0:T(8,128)(2,1)S(1)}, u32[]{:S(2)}, u32[]{:S(2)}) collective-permute-start(bf16[128,512]{1,0:T(8,128)(2,1)S(1)} %convolution_convert_fusion.5), channel_id=1, source_target_pairs={{0,4},{4,8},{8,12},{12,16},{16,20},{20,24},{24,28},{1,5},{5,9},{9,... | collective-permute-start | bytes 393224 | tf_op jit(solution)/shard_map/while/body/eval_jaxpr/ppermute | solution.py:14
  158.1 7.1 %collective-permute-start = (bf16[128,512]{1,0:T(8,128)(2,1)S(1)}, bf16[128,512]{1,0:T(8,128)(2,1)S(1)}, u32[]{:S(2)}, u32[]{:S(2)}) collective-permute-start(bf16[128,512]{1,0:T(8,128)(2,1)S(1)} %convolution_convert_fusion.5), channel_id=1, source_target_pairs={{0,4},{4,8},{8,12},{12,16},{16,20},{20,24},{24,28},{1,5},{5,9},{9,... | collective-permute-start | bytes 393224 | tf_op jit(solution)/shard_map/while/body/eval_jaxpr/ppermute | solution.py:14
  168.0 12.1 %copy-start.3 = (f32[128,2048]{1,0:T(8,128)}, f32[128,2048]{1,0:T(8,128)S(1)}, u32[]{:S(2)}) copy-start(f32[128,2048]{1,0:T(8,128)S(1)} %fusion.72) | copy-start | bytes 3145732
  180.3 7.0 %collective-permute-start.6 = (bf16[128,512]{1,0:T(8,128)(2,1)S(1)}, bf16[128,512]{1,0:T(8,128)(2,1)S(1)}, u32[]{:S(2)}, u32[]{:S(2)}) collective-permute-start(bf16[128,512]{1,0:T(8,128)(2,1)S(1)} %add_convert_fusion.3), channel_id=1, source_target_pairs={{4,0},{8,4},{12,8},{16,12},{20,16},{24,20},{28,24},{5,1},{9,5},{13... | collective-permute-start | bytes 393224 | tf_op jit(solution)/shard_map/ppermute | solution.py:14
  191.7 12.3 %copy-start.2 = (f32[512,512]{1,0:T(8,128)S(1)}, f32[512,512]{1,0:T(8,128)}, u32[]{:S(2)}) copy-start(f32[512,512]{1,0:T(8,128)} %copy-done.1) | copy-start | bytes 3145732
  196.1 7.9 %collective-permute-start.7 = (bf16[128,512]{1,0:T(8,128)(2,1)S(1)}, bf16[128,512]{1,0:T(8,128)(2,1)S(1)}, u32[]{:S(2)}, u32[]{:S(2)}) collective-permute-start(bf16[128,512]{1,0:T(8,128)(2,1)S(1)} %add_convert_fusion.2), channel_id=1, source_target_pairs={{4,0},{8,4},{12,8},{16,12},{20,16},{24,20},{28,24},{5,1},{9,5},{13... | collective-permute-start | bytes 393224 | tf_op jit(solution)/shard_map/ppermute | solution.py:14
  205.8 16.4 %collective-permute-start.9 = (bf16[128,512]{1,0:T(8,128)(2,1)}, bf16[128,512]{1,0:T(8,128)(2,1)}, u32[]{:S(2)}, u32[]{:S(2)}) collective-permute-start(bf16[128,512]{1,0:T(8,128)(2,1)} %convolution_convert_fusion.2), channel_id=1, source_target_pairs={{4,0},{8,4},{12,8},{16,12},{20,16},{24,20},{28,24},{5,1},{9,5},{13... | collective-permute-start | bytes 393224 | tf_op jit(solution)/shard_map/ppermute | solution.py:14
  218.0 7.9 %collective-permute-start.8 = (bf16[128,512]{1,0:T(8,128)(2,1)}, bf16[128,512]{1,0:T(8,128)(2,1)S(1)}, u32[]{:S(2)}, u32[]{:S(2)}) collective-permute-start(bf16[128,512]{1,0:T(8,128)(2,1)} %get-tuple-element.110), channel_id=1, source_target_pairs={{4,0},{8,4},{12,8},{16,12},{20,16},{24,20},{28,24},{5,1},{9,5},{13... | collective-permute-start | bytes 393224 | tf_op jit(solution)/shard_map/ppermute | solution.py:14
  227.6 7.9 %collective-permute-start.1 = (bf16[128,512]{1,0:T(8,128)(2,1)S(1)}, bf16[128,512]{1,0:T(8,128)(2,1)S(1)}, u32[]{:S(2)}, u32[]{:S(2)}) collective-permute-start(bf16[128,512]{1,0:T(8,128)(2,1)S(1)} %convolution_convert_fusion.6), channel_id=1, source_target_pairs={{4,0},{8,4},{12,8},{16,12},{20,16},{24,20},{28,24},{5,1},{9,5},{13... | collective-permute-start | bytes 393224 | tf_op jit(solution)/shard_map/while/body/eval_jaxpr/ppermute | solution.py:14
  236.3 7.2 %collective-permute-start.1 = (bf16[128,512]{1,0:T(8,128)(2,1)S(1)}, bf16[128,512]{1,0:T(8,128)(2,1)S(1)}, u32[]{:S(2)}, u32[]{:S(2)}) collective-permute-start(bf16[128,512]{1,0:T(8,128)(2,1)S(1)} %convolution_convert_fusion.6), channel_id=1, source_target_pairs={{4,0},{8,4},{12,8},{16,12},{20,16},{24,20},{28,24},{5,1},{9,5},{13... | collective-permute-start | bytes 393224 | tf_op jit(solution)/shard_map/while/body/eval_jaxpr/ppermute | solution.py:14
  244.3 7.2 %collective-permute-start.1 = (bf16[128,512]{1,0:T(8,128)(2,1)S(1)}, bf16[128,512]{1,0:T(8,128)(2,1)S(1)}, u32[]{:S(2)}, u32[]{:S(2)}) collective-permute-start(bf16[128,512]{1,0:T(8,128)(2,1)S(1)} %convolution_convert_fusion.6), channel_id=1, source_target_pairs={{4,0},{8,4},{12,8},{16,12},{20,16},{24,20},{28,24},{5,1},{9,5},{13... | collective-permute-start | bytes 393224 | tf_op jit(solution)/shard_map/while/body/eval_jaxpr/ppermute | solution.py:14
  252.2 7.2 %collective-permute-start.1 = (bf16[128,512]{1,0:T(8,128)(2,1)S(1)}, bf16[128,512]{1,0:T(8,128)(2,1)S(1)}, u32[]{:S(2)}, u32[]{:S(2)}) collective-permute-start(bf16[128,512]{1,0:T(8,128)(2,1)S(1)} %convolution_convert_fusion.6), channel_id=1, source_target_pairs={{4,0},{8,4},{12,8},{16,12},{20,16},{24,20},{28,24},{5,1},{9,5},{13... | collective-permute-start | bytes 393224 | tf_op jit(solution)/shard_map/while/body/eval_jaxpr/ppermute | solution.py:14
  260.2 7.2 %collective-permute-start.1 = (bf16[128,512]{1,0:T(8,128)(2,1)S(1)}, bf16[128,512]{1,0:T(8,128)(2,1)S(1)}, u32[]{:S(2)}, u32[]{:S(2)}) collective-permute-start(bf16[128,512]{1,0:T(8,128)(2,1)S(1)} %convolution_convert_fusion.6), channel_id=1, source_target_pairs={{4,0},{8,4},{12,8},{16,12},{20,16},{24,20},{28,24},{5,1},{9,5},{13... | collective-permute-start | bytes 393224 | tf_op jit(solution)/shard_map/while/body/eval_jaxpr/ppermute | solution.py:14
  268.2 7.2 %collective-permute-start.1 = (bf16[128,512]{1,0:T(8,128)(2,1)S(1)}, bf16[128,512]{1,0:T(8,128)(2,1)S(1)}, u32[]{:S(2)}, u32[]{:S(2)}) collective-permute-start(bf16[128,512]{1,0:T(8,128)(2,1)S(1)} %convolution_convert_fusion.6), channel_id=1, source_target_pairs={{4,0},{8,4},{12,8},{16,12},{20,16},{24,20},{28,24},{5,1},{9,5},{13... | collective-permute-start | bytes 393224 | tf_op jit(solution)/shard_map/while/body/eval_jaxpr/ppermute | solution.py:14
  276.1 7.2 %collective-permute-start.1 = (bf16[128,512]{1,0:T(8,128)(2,1)S(1)}, bf16[128,512]{1,0:T(8,128)(2,1)S(1)}, u32[]{:S(2)}, u32[]{:S(2)}) collective-permute-start(bf16[128,512]{1,0:T(8,128)(2,1)S(1)} %convolution_convert_fusion.6), channel_id=1, source_target_pairs={{4,0},{8,4},{12,8},{16,12},{20,16},{24,20},{28,24},{5,1},{9,5},{13... | collective-permute-start | bytes 393224 | tf_op jit(solution)/shard_map/while/body/eval_jaxpr/ppermute | solution.py:14
  289.0 137.8 %all-gather.3.cloned.1.call-start = ((), (), s32[]{:S(2)}) async-start(), calls=%async_computation.3 | async-start | bytes 5242880 | tf_op jit(solution)/shard_map/all_gather | solution.py:131
  291.6 9.2 %copy-start.5 = (f32[128,2048]{1,0:T(8,128)S(1)}, f32[128,2048]{1,0:T(8,128)}, u32[]{:S(2)}) copy-start(f32[128,2048]{1,0:T(8,128)} %fusion.43) | copy-start | bytes 3145732
  296.1 11.5 %all-to-all-start = ((bf16[2,128,512]{1,0,2:T(2,128)(2,1)}), bf16[2,128,512]{1,0,2:T(2,128)(2,1)}, u32[]{:S(2)}, u32[]{:S(2)}) async-start(bf16[2,128,512]{1,0,2:T(2,128)(2,1)} %copy.10), calls=%async_computation | async-start | bytes 524288 | tf_op jit(solution)/shard_map/all_to_all | solution.py:127
  307.6 42.5 %all-to-all-start.1 = ((bf16[2,128,2048]{1,0,2:T(2,128)(2,1)}), bf16[2,128,2048]{1,0,2:T(2,128)(2,1)S(1)}, u32[]{:S(2)}, u32[]{:S(2)}) async-start(bf16[2,128,2048]{1,0,2:T(2,128)(2,1)} %copy.13), calls=%async_computation.1 | async-start | bytes 2097152 | tf_op jit(solution)/shard_map/all_to_all | solution.py:128
  351.3 75.4 %copy-start.8 = (bf16[2,512,128]{1,2,0:T(8,128)(2,1)S(1)}, bf16[2,512,128]{1,2,0:T(8,128)(2,1)}, u32[]{:S(2)}) copy-start(bf16[2,512,128]{1,2,0:T(8,128)(2,1)} %all_to_all.29) | copy-start | bytes 786436
  (11 other events, 31.0 us)
Sparse Core Ops, SparseCore 0:
  11.6 56.1 all-reduce.1
  289.1 52.3 all-gather.4
  343.7 83.0 all-gather.2
where the time goes:
time: 439 us; the launch traced here: 438 us
  waiting for transfers between devices  237 us (54%)
  matrix products  86.1 us (20%)
  starting transfers between devices  74.1 us (17%)
  between operations  14.2 us (3%)
  local copies, waits for them, and re-layouts  13.4 us (3%)
  other arithmetic  12.5 us (3%)
    all_gather x1, waiting for transfers between devices, shards(): lax.all_gather(delta_all, 'dp', axis=1, tiled=True)  72 us
    ppermute x22, starting transfers between devices, shifted(): return lax.ppermute(block, axis, route)  65.9 us
    ppermute x22, waiting for transfers between devices, shifted(): return lax.ppermute(block, axis, route)  65.8 us
    psum x1, waiting for transfers between devices, shards(): start = lax.psum(picked.astype(jnp.bfloat16), 'depth').astype(jnp.float32)  57.6 us
    all_to_all x1, waiting for transfers between devices, shards(): lax.all_to_all(hidden_all, 'dp', split_axis=2, concat_axis=1, tiled=True)  37 us
    dot_general x7, matrix products, layer_adjoint(): lax.dot_general(delta, weight_up, (((1,), (1,)), ((), ())), preferred_ele...  26.4 us
    dot_general x7, matrix products, layer_forward(): jnp.dot(hidden, weight_down, preferred_element_type=jnp.float32)  21.2 us
  transfers between devices with their start and end apart: 27, of which 22 were waited for; matrix products, arithmetic and copies ran while one was open for 9% of the time, Pallas kernels for 0%

commit v1 on v0

--- a/solution.py
+++ b/solution.py
@@ -125,7 +125,12 @@
     low_all = jnp.stack(lows, 0)
     normed_part, hidden_part = (
         lax.all_to_all(normed_all, "dp", split_axis=2, concat_axis=1, tiled=True),
-        lax.all_to_all(hidden_all, "dp", split_axis=2, concat_axis=1, tiled=True),
+        jnp.concatenate(
+            lax.all_to_all(
+                jnp.stack(jnp.split(hidden_all, lax.axis_size("dp"), axis=2)), "dp", 0, 0
+            ),
+            axis=1,
+        ),
     )
     delta_whole, low_whole = (
         lax.all_gather(delta_all, "dp", axis=1, tiled=True),

time: 439 us -> 440 us (level)
  local copies, waits for them, and re-layouts: 13.4 us -> 8.3 us
  waiting for transfers between devices: 237 us -> 242 us
  transfers between devices with their start and end apart: 27 -> 27, of which waited for: 22 -> 22; matrix products, arithmetic and copies ran while one was open for 9% -> 8% of each run, Pallas kernels for 0% -> 0%
where the time goes in v1:
time: 440 us; the launch traced here: 439 us
  waiting for transfers between devices  242 us (55%)
  matrix products  86.7 us (20%)
  starting transfers between devices  74.2 us (17%)
  between operations  14.2 us (3%)
  other arithmetic  13 us (3%)
  local copies, waits for them, and re-layouts  8.3 us (2%)
    all_gather x1, waiting for transfers between devices, shards(): lax.all_gather(delta_all, 'dp', axis=1, tiled=True)  75.2 us
    ppermute x22, starting transfers between devices, shifted(): return lax.ppermute(block, axis, route)  65.9 us
    ppermute x22, waiting for transfers between devices, shifted(): return lax.ppermute(block, axis, route)  65.7 us
    psum x1, waiting for transfers between devices, shards(): start = lax.psum(picked.astype(jnp.bfloat16), 'depth').astype(jnp.float32)  57.6 us
    all_to_all x1, waiting for transfers between devices, shards(): lax.all_to_all(jnp.stack(jnp.split(hidden_all, lax.axis_size('dp'), axis=...  39.5 us
    dot_general x7, matrix products, layer_adjoint(): lax.dot_general(delta, weight_up, (((1,), (1,)), ((), ())), preferred_ele...  27.1 us
    dot_general x7, matrix products, layer_forward(): jnp.dot(hidden, weight_down, preferred_element_type=jnp.float32)  21.2 us
  transfers between devices with their start and end apart: 27, of which 22 were waited for; matrix products, arithmetic and copies ran while one was open for 8% of the time, Pallas kernels for 0%

profile of v1, /device:TPU:0, one launch (start us, length us, event | category | flops | bytes accessed | tf_op | source)
XLA Modules:
  0.0 438.7 jit_solution(4182290960799304382)
XLA Ops:
  10.2 57.6 %all-reduce.2.cloned.1.call-done = bf16[128,512]{1,0:T(8,128)(2,1)} async-done(((bf16[128,512]{1,0:T(8,128)(2,1)}), bf16[128,512]{1,0:T(8,128)(2,1)}) %all-reduce.2.cloned.1.call-update) | async-done | bytes 131088 | tf_op jit(solution)/shard_map/psum | solution.py:59
  76.4 4.4 %fusion.27 = f32[512,512]{1,0:T(8,128)} fusion(bf16[2,2048,512]{2,1,0:T(8,128)(2,1)} %param.12, bf16[2,512,2048]{2,1,0:T(8,128)(2,1)} %param.11), kind=kOutput, calls=%fused_computation.40 | convolution fusion | flops 1073741824 | bytes 5242880 | tf_op jit(solution)/shard_map/dot_general | solution.py:44
  99.7 4.0 fusion.121
  103.6 4.0 collective-permute-start.4
  109.1 4.5 %collective-permute-start.5 = (f32[128,512]{1,0:T(8,128)}, f32[128,512]{1,0:T(8,128)S(1)}, u32[]{:S(2)}, u32[]{:S(2)}) collective-permute-start(f32[128,512]{1,0:T(8,128)} %fusion.251), channel_id=1, source_target_pairs={{0,4},{4,8},{8,12},{12,16},{16,20},{20,24},{24,28},{1,5},{5,9},{9,... | collective-permute-start | bytes 786440 | tf_op jit(solution)/shard_map/ppermute | solution.py:14
  114.8 50.3 %while.22 = (s32[]{:T(128)}, f32[128,512]{1,0:T(8,128)S(1)}, f32[128,512]{1,0:T(8,128)S(1)}, f32[512,512]{1,0:T(8,128)S(1)}, s32[]{:T(128)}, /*index=5*/s32[]{:T(128)}) while((s32[]{:T(128)}, f32[128,512]{1,0:T(8,128)S(1)}, f32[128,512]{1,0:T(8,128)S(1)}, f32[512,512]{1,0:T(8,128)S(1)}, s32[]{:T(128)}, /*index=5*/s32[]{:T(128)}) %tuple.68), condition=%wide.region_8.9_spmd.clone, body=%wide.region_7.8_spmd.clone.sunk | while | flops 402915328 | bytes 2621559 | solution.py:78
  115.6 5.4 %collective-permute-start = (bf16[128,512]{1,0:T(8,128)(2,1)S(1)}, bf16[128,512]{1,0:T(8,128)(2,1)S(1)}, u32[]{:S(2)}, u32[]{:S(2)}) collective-permute-start(bf16[128,512]{1,0:T(8,128)(2,1)S(1)} %convolution_convert_fusion.5), channel_id=1, source_target_pairs={{0,4},{4,8},{8,12},{12,16},{16,20},{20,24},{24,28},{1,5},{5,9},{9,... | collective-permute-start | bytes 393224 | tf_op jit(solution)/shard_map/while/body/eval_jaxpr/ppermute | solution.py:14
  122.8 5.2 %collective-permute-start = (bf16[128,512]{1,0:T(8,128)(2,1)S(1)}, bf16[128,512]{1,0:T(8,128)(2,1)S(1)}, u32[]{:S(2)}, u32[]{:S(2)}) collective-permute-start(bf16[128,512]{1,0:T(8,128)(2,1)S(1)} %convolution_convert_fusion.5), channel_id=1, source_target_pairs={{0,4},{4,8},{8,12},{12,16},{16,20},{20,24},{24,28},{1,5},{5,9},{9,... | collective-permute-start | bytes 393224 | tf_op jit(solution)/shard_map/while/body/eval_jaxpr/ppermute | solution.py:14
  129.8 5.3 %collective-permute-start = (bf16[128,512]{1,0:T(8,128)(2,1)S(1)}, bf16[128,512]{1,0:T(8,128)(2,1)S(1)}, u32[]{:S(2)}, u32[]{:S(2)}) collective-permute-start(bf16[128,512]{1,0:T(8,128)(2,1)S(1)} %convolution_convert_fusion.5), channel_id=1, source_target_pairs={{0,4},{4,8},{8,12},{12,16},{16,20},{20,24},{24,28},{1,5},{5,9},{9,... | collective-permute-start | bytes 393224 | tf_op jit(solution)/shard_map/while/body/eval_jaxpr/ppermute | solution.py:14
  136.8 5.3 %collective-permute-start = (bf16[128,512]{1,0:T(8,128)(2,1)S(1)}, bf16[128,512]{1,0:T(8,128)(2,1)S(1)}, u32[]{:S(2)}, u32[]{:S(2)}) collective-permute-start(bf16[128,512]{1,0:T(8,128)(2,1)S(1)} %convolution_convert_fusion.5), channel_id=1, source_target_pairs={{0,4},{4,8},{8,12},{12,16},{16,20},{20,24},{24,28},{1,5},{5,9},{9,... | collective-permute-start | bytes 393224 | tf_op jit(solution)/shard_map/while/body/eval_jaxpr/ppermute | solution.py:14
  143.9 5.3 %collective-permute-start = (bf16[128,512]{1,0:T(8,128)(2,1)S(1)}, bf16[128,512]{1,0:T(8,128)(2,1)S(1)}, u32[]{:S(2)}, u32[]{:S(2)}) collective-permute-start(bf16[128,512]{1,0:T(8,128)(2,1)S(1)} %convolution_convert_fusion.5), channel_id=1, source_target_pairs={{0,4},{4,8},{8,12},{12,16},{16,20},{20,24},{24,28},{1,5},{5,9},{9,... | collective-permute-start | bytes 393224 | tf_op jit(solution)/shard_map/while/body/eval_jaxpr/ppermute | solution.py:14
  151.0 5.3 %collective-permute-start = (bf16[128,512]{1,0:T(8,128)(2,1)S(1)}, bf16[128,512]{1,0:T(8,128)(2,1)S(1)}, u32[]{:S(2)}, u32[]{:S(2)}) collective-permute-start(bf16[128,512]{1,0:T(8,128)(2,1)S(1)} %convolution_convert_fusion.5), channel_id=1, source_target_pairs={{0,4},{4,8},{8,12},{12,16},{16,20},{20,24},{24,28},{1,5},{5,9},{9,... | collective-permute-start | bytes 393224 | tf_op jit(solution)/shard_map/while/body/eval_jaxpr/ppermute | solution.py:14
  158.0 6.2 %collective-permute-start = (bf16[128,512]{1,0:T(8,128)(2,1)S(1)}, bf16[128,512]{1,0:T(8,128)(2,1)S(1)}, u32[]{:S(2)}, u32[]{:S(2)}) collective-permute-start(bf16[128,512]{1,0:T(8,128)(2,1)S(1)} %convolution_convert_fusion.5), channel_id=1, source_target_pairs={{0,4},{4,8},{8,12},{12,16},{16,20},{20,24},{24,28},{1,5},{5,9},{9,... | collective-permute-start | bytes 393224 | tf_op jit(solution)/shard_map/while/body/eval_jaxpr/ppermute | solution.py:14
  172.0 4.2 multiply_reduce_fusion.6
  181.6 5.7 %collective-permute-done.6 = bf16[128,512]{1,0:T(8,128)(2,1)S(1)} collective-permute-done((bf16[128,512]{1,0:T(8,128)(2,1)S(1)}, bf16[128,512]{1,0:T(8,128)(2,1)S(1)}, u32[]{:S(2)}, u32[]{:S(2)}) %collective-permute-start.6) | collective-permute-done | bytes 131104 | tf_op jit(solution)/shard_map/ppermute | solution.py:14
  187.4 4.2 multiply_reduce_fusion.4
  191.7 4.3 multiply_reduce_fusion.3
  197.4 6.6 %collective-permute-done.7 = bf16[128,512]{1,0:T(8,128)(2,1)S(1)} collective-permute-done((bf16[128,512]{1,0:T(8,128)(2,1)S(1)}, bf16[128,512]{1,0:T(8,128)(2,1)S(1)}, u32[]{:S(2)}, u32[]{:S(2)}) %collective-permute-start.7) | collective-permute-done | bytes 131104 | tf_op jit(solution)/shard_map/ppermute | solution.py:14
  207.1 4.8 %multiply_reduce_fusion.2 = (f32[128]{0:T(128)S(1)}, f32[128,512]{1,0:T(8,128)}) fusion(f32[128,512]{1,0:T(8,128)S(1)} %get-tuple-element.130, f32[128]{0:T(128)S(1)} %add_rsqrt_fusion, bf16[2,512,2048]{2,1,0:T(8,128)(2,1)} %param.11, f32[128,2048]{1,0:T(8,128)} %fusion.43, bf16[2,2048,512]{2,1,0:T(8,128)(2,1)} %param.12, ...), kind=kOutput, calls=%fused_computation.186 | convolution fusion | flops 539688832 | bytes 6030337 | tf_op jit(solution)/shard_map/dot_general | solution.py:34
  213.0 4.8 %multiply_reduce_fusion.1 = (f32[128]{0:T(128)S(1)}, f32[128,512]{1,0:T(8,128)}) fusion(f32[128,512]{1,0:T(8,128)S(1)} %get-tuple-element.109, f32[128]{0:T(128)S(1)} %add_rsqrt_fusion.1, bf16[2,512,2048]{2,1,0:T(8,128)(2,1)} %param.11, f32[128,2048]{1,0:T(8,128)} %copy-done.3, f32[128,512]{1,0:T(8,128)S(1)} %multiply_add_fusion.8, ...), kind=kOutput, calls=%fused_computation.184 | convolution fusion | flops 539492224 | bytes 6030336 | tf_op jit(solution)/shard_map/dot_general | solution.py:34
  227.8 56.4 %while.23 = (s32[]{:T(128)}, f32[128,512]{1,0:T(8,128)S(1)}, f32[128,512]{1,0:T(8,128)S(1)}, f32[512,512]{1,0:T(8,128)S(1)}, s32[]{:T(128)}, /*index=5*/s32[]{:T(128)}) while((s32[]{:T(128)}, f32[128,512]{1,0:T(8,128)S(1)}, f32[128,512]{1,0:T(8,128)S(1)}, f32[512,512]{1,0:T(8,128)S(1)}, s32[]{:T(128)}, ...), condition=%wide.region_18.19_spmd.clone, body=%wide.region_17.18_spmd.clone.sunk | while | flops 402915328 | bytes 2621559 | solution.py:112
  229.9 6.6 %collective-permute-done.1 = bf16[128,512]{1,0:T(8,128)(2,1)S(1)} collective-permute-done((bf16[128,512]{1,0:T(8,128)(2,1)S(1)}, bf16[128,512]{1,0:T(8,128)(2,1)S(1)}, u32[]{:S(2)}, u32[]{:S(2)}) %collective-permute-start.1) | collective-permute-done | bytes 131104 | tf_op jit(solution)/shard_map/while/body/eval_jaxpr/ppermute | solution.py:14
  238.5 5.9 %collective-permute-done.1 = bf16[128,512]{1,0:T(8,128)(2,1)S(1)} collective-permute-done((bf16[128,512]{1,0:T(8,128)(2,1)S(1)}, bf16[128,512]{1,0:T(8,128)(2,1)S(1)}, u32[]{:S(2)}, u32[]{:S(2)}) %collective-permute-start.1) | collective-permute-done | bytes 131104 | tf_op jit(solution)/shard_map/while/body/eval_jaxpr/ppermute | solution.py:14
  246.5 5.9 %collective-permute-done.1 = bf16[128,512]{1,0:T(8,128)(2,1)S(1)} collective-permute-done((bf16[128,512]{1,0:T(8,128)(2,1)S(1)}, bf16[128,512]{1,0:T(8,128)(2,1)S(1)}, u32[]{:S(2)}, u32[]{:S(2)}) %collective-permute-start.1) | collective-permute-done | bytes 131104 | tf_op jit(solution)/shard_map/while/body/eval_jaxpr/ppermute | solution.py:14
  254.4 5.9 %collective-permute-done.1 = bf16[128,512]{1,0:T(8,128)(2,1)S(1)} collective-permute-done((bf16[128,512]{1,0:T(8,128)(2,1)S(1)}, bf16[128,512]{1,0:T(8,128)(2,1)S(1)}, u32[]{:S(2)}, u32[]{:S(2)}) %collective-permute-start.1) | collective-permute-done | bytes 131104 | tf_op jit(solution)/shard_map/while/body/eval_jaxpr/ppermute | solution.py:14
  262.4 5.9 %collective-permute-done.1 = bf16[128,512]{1,0:T(8,128)(2,1)S(1)} collective-permute-done((bf16[128,512]{1,0:T(8,128)(2,1)S(1)}, bf16[128,512]{1,0:T(8,128)(2,1)S(1)}, u32[]{:S(2)}, u32[]{:S(2)}) %collective-permute-start.1) | collective-permute-done | bytes 131104 | tf_op jit(solution)/shard_map/while/body/eval_jaxpr/ppermute | solution.py:14
  270.4 5.9 %collective-permute-done.1 = bf16[128,512]{1,0:T(8,128)(2,1)S(1)} collective-permute-done((bf16[128,512]{1,0:T(8,128)(2,1)S(1)}, bf16[128,512]{1,0:T(8,128)(2,1)S(1)}, u32[]{:S(2)}, u32[]{:S(2)}) %collective-permute-start.1) | collective-permute-done | bytes 131104 | tf_op jit(solution)/shard_map/while/body/eval_jaxpr/ppermute | solution.py:14
  278.3 5.9 %collective-permute-done.1 = bf16[128,512]{1,0:T(8,128)(2,1)S(1)} collective-permute-done((bf16[128,512]{1,0:T(8,128)(2,1)S(1)}, bf16[128,512]{1,0:T(8,128)(2,1)S(1)}, u32[]{:S(2)}, u32[]{:S(2)}) %collective-permute-start.1) | collective-permute-done | bytes 131104 | tf_op jit(solution)/shard_map/while/body/eval_jaxpr/ppermute | solution.py:14
  293.9 4.6 %all-to-all-start = ((bf16[2,128,512]{1,0,2:T(2,128)(2,1)}), bf16[2,128,512]{1,0,2:T(2,128)(2,1)S(1)}, u32[]{:S(2)}, u32[]{:S(2)}) async-start(bf16[2,128,512]{1,0,2:T(2,128)(2,1)} %copy.13), calls=%async_computation | async-start | bytes 524288 | tf_op jit(solution)/shard_map/all_to_all | solution.py:127
  309.8 39.5 %all-to-all-done.1 = bf16[4,2,128,512]{3,2,1,0:T(8,128)(2,1)S(1)} async-done(((bf16[4,2,128,512]{3,2,1,0:T(8,128)(2,1)}), bf16[4,2,128,512]{3,2,1,0:T(8,128)(2,1)S(1)}, u32[]{:S(2)}, u32[]{:S(2)}) %all-to-all-start.1) | async-done | bytes 1048608 | tf_op jit(solution)/shard_map/all_to_all | solution.py:129
  352.8 75.2 %all-gather.3.cloned.1.call-done = bf16[2,512,2048]{2,1,0:T(8,128)(2,1)} async-done(((bf16[2,128,2048]{2,1,0:T(8,128)(2,1)}), bf16[2,512,2048]{2,1,0:T(8,128)(2,1)}) %all-gather.3.cloned.1.call-update) | async-done | bytes 4194320 | tf_op jit(solution)/shard_map/all_gather | solution.py:136
  428.0 4.2 fusion.298
  (153 shorter events, 111.4 us)
Async XLA Ops:
  7.2 60.6 %all-reduce.2.cloned.1.call-start = ((), (), s32[]{:S(2)}) async-start(), calls=%async_computation.2 | async-start | bytes 262144 | tf_op jit(solution)/shard_map/psum | solution.py:59
  10.1 339.3 %all-gather.5.cloned.1.call-start = ((), (), s32[]{:S(2)}) async-start(), calls=%async_computation.4 | async-start | bytes 1310720 | tf_op jit(solution)/shard_map/all_gather | solution.py:137
  75.0 5.9 %copy-start.8 = (bf16[128,512]{1,0:T(8,128)(2,1)S(1)}, bf16[128,512]{1,0:T(8,128)(2,1)}, u32[]{:S(2)}) copy-start(bf16[128,512]{1,0:T(8,128)(2,1)} %all-reduce.2.cloned.1.call-done) | copy-start | bytes 393220
  75.0 5.9 %collective-permute-start.2 = (f32[128,512]{1,0:T(8,128)S(1)}, f32[128,512]{1,0:T(8,128)S(1)}, u32[]{:S(2)}, u32[]{:S(2)}) collective-permute-start(f32[128,512]{1,0:T(8,128)S(1)} %fusion.115), channel_id=1, source_target_pairs={{0,4},{4,8},{8,12},{12,16},{16,20},{20,24},{24,28},{1,5},{5,9},{9,... | collective-permute-start | bytes 786440 | tf_op jit(solution)/shard_map/ppermute | solution.py:14
  87.8 7.2 %collective-permute-start.3 = (f32[128,512]{1,0:T(8,128)}, f32[128,512]{1,0:T(8,128)S(1)}, u32[]{:S(2)}, u32[]{:S(2)}) collective-permute-start(f32[128,512]{1,0:T(8,128)} %fusion.118), channel_id=1, source_target_pairs={{0,4},{4,8},{8,12},{12,16},{16,20},{20,24},{24,28},{1,5},{5,9},{9,... | collective-permute-start | bytes 786440 | tf_op jit(solution)/shard_map/ppermute | solution.py:14
  95.0 12.6 %copy-start.1 = (f32[512,512]{1,0:T(8,128)}, f32[512,512]{1,0:T(8,128)S(1)}, u32[]{:S(2)}) copy-start(f32[512,512]{1,0:T(8,128)S(1)} %get-tuple-element.128) | copy-start | bytes 3145732
  103.6 10.0 %collective-permute-start.4 = (f32[128,512]{1,0:T(8,128)}, f32[128,512]{1,0:T(8,128)}, u32[]{:S(2)}, u32[]{:S(2)}) collective-permute-start(f32[128,512]{1,0:T(8,128)} %fusion.121), channel_id=1, source_target_pairs={{0,4},{4,8},{8,12},{12,16},{16,20},{20,24},{24,28},{1,5},{5,9},{9,... | collective-permute-start | bytes 786440 | tf_op jit(solution)/shard_map/ppermute | solution.py:14
  109.1 5.7 %collective-permute-start.5 = (f32[128,512]{1,0:T(8,128)}, f32[128,512]{1,0:T(8,128)S(1)}, u32[]{:S(2)}, u32[]{:S(2)}) collective-permute-start(f32[128,512]{1,0:T(8,128)} %fusion.251), channel_id=1, source_target_pairs={{0,4},{4,8},{8,12},{12,16},{16,20},{20,24},{24,28},{1,5},{5,9},{9,... | collective-permute-start | bytes 786440 | tf_op jit(solution)/shard_map/ppermute | solution.py:14
  115.6 6.4 %collective-permute-start = (bf16[128,512]{1,0:T(8,128)(2,1)S(1)}, bf16[128,512]{1,0:T(8,128)(2,1)S(1)}, u32[]{:S(2)}, u32[]{:S(2)}) collective-permute-start(bf16[128,512]{1,0:T(8,128)(2,1)S(1)} %convolution_convert_fusion.5), channel_id=1, source_target_pairs={{0,4},{4,8},{8,12},{12,16},{16,20},{20,24},{24,28},{1,5},{5,9},{9,... | collective-permute-start | bytes 393224 | tf_op jit(solution)/shard_map/while/body/eval_jaxpr/ppermute | solution.py:14
  122.8 6.2 %collective-permute-start = (bf16[128,512]{1,0:T(8,128)(2,1)S(1)}, bf16[128,512]{1,0:T(8,128)(2,1)S(1)}, u32[]{:S(2)}, u32[]{:S(2)}) collective-permute-start(bf16[128,512]{1,0:T(8,128)(2,1)S(1)} %convolution_convert_fusion.5), channel_id=1, source_target_pairs={{0,4},{4,8},{8,12},{12,16},{16,20},{20,24},{24,28},{1,5},{5,9},{9,... | collective-permute-start | bytes 393224 | tf_op jit(solution)/shard_map/while/body/eval_jaxpr/ppermute | solution.py:14
  129.8 6.3 %collective-permute-start = (bf16[128,512]{1,0:T(8,128)(2,1)S(1)}, bf16[128,512]{1,0:T(8,128)(2,1)S(1)}, u32[]{:S(2)}, u32[]{:S(2)}) collective-permute-start(bf16[128,512]{1,0:T(8,128)(2,1)S(1)} %convolution_convert_fusion.5), channel_id=1, source_target_pairs={{0,4},{4,8},{8,12},{12,16},{16,20},{20,24},{24,28},{1,5},{5,9},{9,... | collective-permute-start | bytes 393224 | tf_op jit(solution)/shard_map/while/body/eval_jaxpr/ppermute | solution.py:14
  136.8 6.3 %collective-permute-start = (bf16[128,512]{1,0:T(8,128)(2,1)S(1)}, bf16[128,512]{1,0:T(8,128)(2,1)S(1)}, u32[]{:S(2)}, u32[]{:S(2)}) collective-permute-start(bf16[128,512]{1,0:T(8,128)(2,1)S(1)} %convolution_convert_fusion.5), channel_id=1, source_target_pairs={{0,4},{4,8},{8,12},{12,16},{16,20},{20,24},{24,28},{1,5},{5,9},{9,... | collective-permute-start | bytes 393224 | tf_op jit(solution)/shard_map/while/body/eval_jaxpr/ppermute | solution.py:14
  143.9 6.3 %collective-permute-start = (bf16[128,512]{1,0:T(8,128)(2,1)S(1)}, bf16[128,512]{1,0:T(8,128)(2,1)S(1)}, u32[]{:S(2)}, u32[]{:S(2)}) collective-permute-start(bf16[128,512]{1,0:T(8,128)(2,1)S(1)} %convolution_convert_fusion.5), channel_id=1, source_target_pairs={{0,4},{4,8},{8,12},{12,16},{16,20},{20,24},{24,28},{1,5},{5,9},{9,... | collective-permute-start | bytes 393224 | tf_op jit(solution)/shard_map/while/body/eval_jaxpr/ppermute | solution.py:14
  151.0 6.3 %collective-permute-start = (bf16[128,512]{1,0:T(8,128)(2,1)S(1)}, bf16[128,512]{1,0:T(8,128)(2,1)S(1)}, u32[]{:S(2)}, u32[]{:S(2)}) collective-permute-start(bf16[128,512]{1,0:T(8,128)(2,1)S(1)} %convolution_convert_fusion.5), channel_id=1, source_target_pairs={{0,4},{4,8},{8,12},{12,16},{16,20},{20,24},{24,28},{1,5},{5,9},{9,... | collective-permute-start | bytes 393224 | tf_op jit(solution)/shard_map/while/body/eval_jaxpr/ppermute | solution.py:14
  158.0 7.1 %collective-permute-start = (bf16[128,512]{1,0:T(8,128)(2,1)S(1)}, bf16[128,512]{1,0:T(8,128)(2,1)S(1)}, u32[]{:S(2)}, u32[]{:S(2)}) collective-permute-start(bf16[128,512]{1,0:T(8,128)(2,1)S(1)} %convolution_convert_fusion.5), channel_id=1, source_target_pairs={{0,4},{4,8},{8,12},{12,16},{16,20},{20,24},{24,28},{1,5},{5,9},{9,... | collective-permute-start | bytes 393224 | tf_op jit(solution)/shard_map/while/body/eval_jaxpr/ppermute | solution.py:14
  168.0 8.2 %copy-start.3 = (f32[128,2048]{1,0:T(8,128)}, f32[128,2048]{1,0:T(8,128)S(1)}, u32[]{:S(2)}) copy-start(f32[128,2048]{1,0:T(8,128)S(1)} %fusion.72) | copy-start | bytes 3145732
  180.3 7.0 %collective-permute-start.6 = (bf16[128,512]{1,0:T(8,128)(2,1)S(1)}, bf16[128,512]{1,0:T(8,128)(2,1)S(1)}, u32[]{:S(2)}, u32[]{:S(2)}) collective-permute-start(bf16[128,512]{1,0:T(8,128)(2,1)S(1)} %add_convert_fusion.3), channel_id=1, source_target_pairs={{4,0},{8,4},{12,8},{16,12},{20,16},{24,20},{28,24},{5,1},{9,5},{13... | collective-permute-start | bytes 393224 | tf_op jit(solution)/shard_map/ppermute | solution.py:14
  191.7 12.3 %copy-start.2 = (f32[512,512]{1,0:T(8,128)S(1)}, f32[512,512]{1,0:T(8,128)}, u32[]{:S(2)}) copy-start(f32[512,512]{1,0:T(8,128)} %copy-done.1) | copy-start | bytes 3145732
  196.1 7.9 %collective-permute-start.7 = (bf16[128,512]{1,0:T(8,128)(2,1)S(1)}, bf16[128,512]{1,0:T(8,128)(2,1)S(1)}, u32[]{:S(2)}, u32[]{:S(2)}) collective-permute-start(bf16[128,512]{1,0:T(8,128)(2,1)S(1)} %add_convert_fusion.2), channel_id=1, source_target_pairs={{4,0},{8,4},{12,8},{16,12},{20,16},{24,20},{28,24},{5,1},{9,5},{13... | collective-permute-start | bytes 393224 | tf_op jit(solution)/shard_map/ppermute | solution.py:14
  205.8 17.3 %collective-permute-start.9 = (bf16[128,512]{1,0:T(8,128)(2,1)}, bf16[128,512]{1,0:T(8,128)(2,1)}, u32[]{:S(2)}, u32[]{:S(2)}) collective-permute-start(bf16[128,512]{1,0:T(8,128)(2,1)} %convolution_convert_fusion.2), channel_id=1, source_target_pairs={{4,0},{8,4},{12,8},{16,12},{20,16},{24,20},{28,24},{5,1},{9,5},{13... | collective-permute-start | bytes 393224 | tf_op jit(solution)/shard_map/ppermute | solution.py:14
  219.0 7.8 %collective-permute-start.8 = (bf16[128,512]{1,0:T(8,128)(2,1)S(1)}, bf16[128,512]{1,0:T(8,128)(2,1)}, u32[]{:S(2)}, u32[]{:S(2)}) collective-permute-start(bf16[128,512]{1,0:T(8,128)(2,1)S(1)} %get-tuple-element.118), channel_id=1, source_target_pairs={{4,0},{8,4},{12,8},{16,12},{20,16},{24,20},{28,24},{5,1},{9,5},{13... | collective-permute-start | bytes 393224 | tf_op jit(solution)/shard_map/ppermute | solution.py:14
  228.6 7.9 %collective-permute-start.1 = (bf16[128,512]{1,0:T(8,128)(2,1)S(1)}, bf16[128,512]{1,0:T(8,128)(2,1)S(1)}, u32[]{:S(2)}, u32[]{:S(2)}) collective-permute-start(bf16[128,512]{1,0:T(8,128)(2,1)S(1)} %convolution_convert_fusion.6), channel_id=1, source_target_pairs={{4,0},{8,4},{12,8},{16,12},{20,16},{24,20},{28,24},{5,1},{9,5},{13... | collective-permute-start | bytes 393224 | tf_op jit(solution)/shard_map/while/body/eval_jaxpr/ppermute | solution.py:14
  237.2 7.2 %collective-permute-start.1 = (bf16[128,512]{1,0:T(8,128)(2,1)S(1)}, bf16[128,512]{1,0:T(8,128)(2,1)S(1)}, u32[]{:S(2)}, u32[]{:S(2)}) collective-permute-start(bf16[128,512]{1,0:T(8,128)(2,1)S(1)} %convolution_convert_fusion.6), channel_id=1, source_target_pairs={{4,0},{8,4},{12,8},{16,12},{20,16},{24,20},{28,24},{5,1},{9,5},{13... | collective-permute-start | bytes 393224 | tf_op jit(solution)/shard_map/while/body/eval_jaxpr/ppermute | solution.py:14
  245.2 7.2 %collective-permute-start.1 = (bf16[128,512]{1,0:T(8,128)(2,1)S(1)}, bf16[128,512]{1,0:T(8,128)(2,1)S(1)}, u32[]{:S(2)}, u32[]{:S(2)}) collective-permute-start(bf16[128,512]{1,0:T(8,128)(2,1)S(1)} %convolution_convert_fusion.6), channel_id=1, source_target_pairs={{4,0},{8,4},{12,8},{16,12},{20,16},{24,20},{28,24},{5,1},{9,5},{13... | collective-permute-start | bytes 393224 | tf_op jit(solution)/shard_map/while/body/eval_jaxpr/ppermute | solution.py:14
  253.1 7.2 %collective-permute-start.1 = (bf16[128,512]{1,0:T(8,128)(2,1)S(1)}, bf16[128,512]{1,0:T(8,128)(2,1)S(1)}, u32[]{:S(2)}, u32[]{:S(2)}) collective-permute-start(bf16[128,512]{1,0:T(8,128)(2,1)S(1)} %convolution_convert_fusion.6), channel_id=1, source_target_pairs={{4,0},{8,4},{12,8},{16,12},{20,16},{24,20},{28,24},{5,1},{9,5},{13... | collective-permute-start | bytes 393224 | tf_op jit(solution)/shard_map/while/body/eval_jaxpr/ppermute | solution.py:14
  261.1 7.2 %collective-permute-start.1 = (bf16[128,512]{1,0:T(8,128)(2,1)S(1)}, bf16[128,512]{1,0:T(8,128)(2,1)S(1)}, u32[]{:S(2)}, u32[]{:S(2)}) collective-permute-start(bf16[128,512]{1,0:T(8,128)(2,1)S(1)} %convolution_convert_fusion.6), channel_id=1, source_target_pairs={{4,0},{8,4},{12,8},{16,12},{20,16},{24,20},{28,24},{5,1},{9,5},{13... | collective-permute-start | bytes 393224 | tf_op jit(solution)/shard_map/while/body/eval_jaxpr/ppermute | solution.py:14
  269.1 7.2 %collective-permute-start.1 = (bf16[128,512]{1,0:T(8,128)(2,1)S(1)}, bf16[128,512]{1,0:T(8,128)(2,1)S(1)}, u32[]{:S(2)}, u32[]{:S(2)}) collective-permute-start(bf16[128,512]{1,0:T(8,128)(2,1)S(1)} %convolution_convert_fusion.6), channel_id=1, source_target_pairs={{4,0},{8,4},{12,8},{16,12},{20,16},{24,20},{28,24},{5,1},{9,5},{13... | collective-permute-start | bytes 393224 | tf_op jit(solution)/shard_map/while/body/eval_jaxpr/ppermute | solution.py:14
  277.0 7.2 %collective-permute-start.1 = (bf16[128,512]{1,0:T(8,128)(2,1)S(1)}, bf16[128,512]{1,0:T(8,128)(2,1)S(1)}, u32[]{:S(2)}, u32[]{:S(2)}) collective-permute-start(bf16[128,512]{1,0:T(8,128)(2,1)S(1)} %convolution_convert_fusion.6), channel_id=1, source_target_pairs={{4,0},{8,4},{12,8},{16,12},{20,16},{24,20},{28,24},{5,1},{9,5},{13... | collective-permute-start | bytes 393224 | tf_op jit(solution)/shard_map/while/body/eval_jaxpr/ppermute | solution.py:14
  289.3 138.7 %all-gather.3.cloned.1.call-start = ((), (), s32[]{:S(2)}) async-start(), calls=%async_computation.3 | async-start | bytes 5242880 | tf_op jit(solution)/shard_map/all_gather | solution.py:136
  293.9 11.4 %all-to-all-start = ((bf16[2,128,512]{1,0,2:T(2,128)(2,1)}), bf16[2,128,512]{1,0,2:T(2,128)(2,1)S(1)}, u32[]{:S(2)}, u32[]{:S(2)}) async-start(bf16[2,128,512]{1,0,2:T(2,128)(2,1)} %copy.13), calls=%async_computation | async-start | bytes 524288 | tf_op jit(solution)/shard_map/all_to_all | solution.py:127
  305.3 44.1 %all-to-all-start.1 = ((bf16[4,2,128,512]{3,2,1,0:T(8,128)(2,1)}), bf16[4,2,128,512]{3,2,1,0:T(8,128)(2,1)S(1)}, u32[]{:S(2)}, u32[]{:S(2)}) async-start(bf16[4,2,128,512]{3,2,1,0:T(8,128)(2,1)} %pad_maximum_fusion.1), calls=%async_computation.1 | async-start | bytes 2097152 | tf_op jit(solution)/shard_map/all_to_all | solution.py:129
  349.4 78.6 %copy-start.7 = (bf16[2,512,128]{1,2,0:T(8,128)(2,1)S(1)}, bf16[2,512,128]{1,2,0:T(8,128)(2,1)}, u32[]{:S(2)}) copy-start(bf16[2,512,128]{1,2,0:T(8,128)(2,1)} %all_to_all.19) | copy-start | bytes 786436
  (9 other events, 20.1 us)
Sparse Core Ops, SparseCore 0:
  11.6 56.1 all-reduce.1
  289.4 55.8 all-gather.4
  347.4 80.5 all-gather.2
